TPU v7x, 768 devices: a whole 4x8x12 slice. The times are simulated.
768 devices in a mesh: chan: 96 (over z, x, core), kred: 8 (over y).
Axes of the slice: x: 4, y: 8, z: 12, core: 2. Of those that a mesh axis runs over, the one named last changes fastest.
Arguments:
- t2_ph: bfloat16 [96, 4096, 128], P('chan', 'kred'), may hold values from -6 to 6
- dest_owner: int32 [96, 4096], P('chan', 'kred'), may hold values from 0 to 95, as said below
- source_owner: int32 [96, 4096], P('chan', 'kred'), may hold values from 0 to 95, as said below
- source_slot: int32 [96, 4096], P('chan', 'kred'), may hold values from 0 to 9
- hole_count: int32 [96], P('chan'), may hold values from 32 to 128
- ladder_v: bfloat16 [96, 4096, 4096], P('chan', None, 'kred'), as said below
Outputs:
- ladder_out: bfloat16 [96, 4096, 128], P('chan', 'kred')
Inputs may be any that keep to these rules, and one draw needn't show every extreme that they name: Within each aligned block of 512 rows of dest_owner[s] at most 10 rows name the same channel, and some channel is named by exactly 10; every channel is named by exactly 512 rows of the same block index over all s. The pairs (source_owner, source_slot) of one channel and one aligned block of 512 columns are distinct and name exactly the rows that dest_owner sends to that channel from that block. `ladder_v`: symmetric in its last two dimensions for each channel.
All inputs are finite; a program needn't handle non-finite values.
Results may differ from a plain program's by a relative error of at most 0.001.
Values may be sent and summed in bfloat16 or wider, within the bound.
No kernel may reach another device: no remote copies, remote signals or barrier semaphores. Data moves between devices by JAX's collectives and lax.ppermute only.
A program may use at most 32 MiB of HBM per device.

v0:
```python
import jax
import jax.numpy as jnp
from jax import lax
from jax.sharding import PartitionSpec as P


def on_device(t2_ph, dest_owner, source_owner, source_slot, hole_count, ladder_v):
    ph_rows = t2_ph[0]
    owners = dest_owner[0]
    owners_count = lax.axis_size("chan")
    slab_rows = ph_rows.shape[0]
    hole_width = ph_rows.shape[1]
    capacity = 2 * slab_rows // owners_count
    matches = (owners[:, None] == jnp.arange(owners_count, dtype=jnp.int32)[None, :]).astype(
        jnp.int32
    )
    before = jnp.sum((jnp.cumsum(matches, axis=0) - matches) * matches, axis=1)
    target = owners * capacity + before
    outbox = jnp.zeros((owners_count * capacity, hole_width), ph_rows.dtype).at[target].set(ph_rows)
    arrived = lax.all_to_all(
        outbox.reshape(owners_count, capacity, hole_width),
        "chan",
        split_axis=0,
        concat_axis=0,
        tiled=True,
    )
    picked = source_owner[0] * capacity + source_slot[0]
    recoupled = arrived.reshape(owners_count * capacity, hole_width)[picked]
    weights = ladder_v[0]
    ladder = lax.psum_scatter(
        jnp.dot(weights, recoupled, preferred_element_type=jnp.float32),
        "kred",
        scatter_dimension=0,
        tiled=True,
    )
    columns = jnp.arange(hole_width, dtype=jnp.int32)
    masked = jnp.where(columns[None, :] < hole_count[0], ladder, jnp.float32(0.0))
    return masked.astype(jnp.bfloat16)[None]


def solution(mesh):
    placed = (
        P("chan", "kred", None),
        P("chan", "kred"),
        P("chan", "kred"),
        P("chan", "kred"),
        P("chan"),
        P("chan", None, "kred"),
    )
    return jax.shard_map(
        on_device, mesh=mesh, in_specs=placed, out_specs=P("chan", "kred", None), check_vma=False
    )
```

profile of v0, /device:TPU:2, one launch (start us, length us, event | category | flops | bytes accessed | tf_op | source)
XLA Modules:
  0.0 110.7 jit_solution(12522617460023459930)
XLA Ops:
  6.5 0.0 copy-start
  6.5 0.7 fusion.4
  7.3 1.3 %reduce-window.6 = s32[96,4,128]{2,0,1:T(8,128)S(1)} reduce-window(s32[96,4,128]{2,0,1:T(8,128)S(1)} %fusion.4, s32[]{:T(128)} %constant.3.clone.1), window={size=1x1x128 pad=0_0x0_0x127_0}, to_apply=%region_0.0 | reduce-window | flops 6242304 | bytes 393220 | tf_op jit(solution)/shard_map/reduce-window
  8.5 0.2 slice_reduce_fusion
  8.8 0.8 fusion.3
  9.6 0.7 compare_select_fusion.1
  10.3 0.0 copy-done
  10.3 1.8 %scatter_custom_fusion = bf16[960,128]{1,0:T(8,128)(2,1)S(1)} fusion(s32[512]{0:T(512)S(1)} %bitcast.47, bf16[1,512,128]{2,1,0:T(8,128)(2,1)S(1)} %copy-done, bf16[]{:T(256)} %constant.5.clone.1), kind=kCustom, calls=%fused_computation.15 | custom fusion | bytes 376834 | tf_op jit(solution)/shard_map/scatter | solution.py:19
  12.1 0.8 reshape.89
  13.0 19.1 %all-to-all-start = ((bf16[96,10,128]{2,1,0:T(8,128)(2,1)}), bf16[96,10,128]{2,1,0:T(8,128)(2,1)S(1)}, u32[]{:S(2)}, u32[]{:S(2)}) async-start(bf16[96,10,128]{2,1,0:T(8,128)(2,1)} %reshape.89), calls=%async_computation | async-start | bytes 786432 | tf_op jit(solution)/shard_map/all_to_all | solution.py:20
  32.0 0.0 reduce-scatter.2.cloned.1.call-start
  32.1 0.7 compare_select_fusion
  32.8 20.7 %all-to-all-done = bf16[96,10,128]{2,1,0:T(8,128)(2,1)S(1)} async-done(((bf16[96,10,128]{2,1,0:T(8,128)(2,1)}), bf16[96,10,128]{2,1,0:T(8,128)(2,1)S(1)}, u32[]{:S(2)}, u32[]{:S(2)}) %all-to-all-start) | async-done | bytes 245792 | tf_op jit(solution)/shard_map/all_to_all | solution.py:20
  53.5 0.1 reshape.90
  53.6 1.3 %gather_fusion = bf16[512,128]{1,0:T(8,128)(2,1)S(1)} fusion(bf16[960,128]{1,0:T(8,128)(2,1)S(1)} %reshape.90, s32[1024]{0:T(1024)S(1)} %pad_clamp_fusion), kind=kCustom, calls=%fused_computation | custom fusion | bytes 264192 | tf_op jit(solution)/shard_map/gather | solution.py:28
  54.9 5.0 %convolution_bitcast_fusion = f32[4096,128]{0,1:T(8,128)} fusion(bf16[512,128]{1,0:T(8,128)(2,1)S(1)} %gather_fusion, bf16[1,4096,512]{2,1,0:T(8,128)(2,1)} %param.11), kind=kOutput, calls=%fused_computation.2 | convolution fusion | flops 536870912 | bytes 6422528 | tf_op jit(solution)/shard_map/dot_general | solution.py:31
  60.0 0.0 reduce-scatter.2.cloned.1.call-update
  60.6 41.4 %reduce-scatter.2.cloned.1.call-done = f32[512,128]{0,1:T(8,128)} async-done(((f32[4096,128]{0,1:T(8,128)}), f32[512,128]{0,1:T(8,128)}) %reduce-scatter.2.cloned.1.call-update) | async-done | bytes 262160 | tf_op jit(solution)/shard_map/reduce_scatter | solution.py:30
  102.0 1.0 fusion.5
  103.1 0.8 copy.9
  (4 shorter events, 0.1 us)
Async XLA Ops:
  6.5 3.8 %copy-start = (bf16[1,512,128]{2,1,0:T(8,128)(2,1)S(1)}, bf16[1,512,128]{2,1,0:T(8,128)(2,1)}, u32[]{:S(2)}) copy-start(bf16[1,512,128]{2,1,0:T(8,128)(2,1)} %param.6) | copy-start | bytes 393220
  13.0 40.5 %all-to-all-start = ((bf16[96,10,128]{2,1,0:T(8,128)(2,1)}), bf16[96,10,128]{2,1,0:T(8,128)(2,1)S(1)}, u32[]{:S(2)}, u32[]{:S(2)}) async-start(bf16[96,10,128]{2,1,0:T(8,128)(2,1)} %reshape.89), calls=%async_computation | async-start | bytes 786432 | tf_op jit(solution)/shard_map/all_to_all | solution.py:20
  32.0 70.0 %reduce-scatter.2.cloned.1.call-start = ((), (), s32[]{:S(2)}) async-start(), calls=%async_computation.2 | async-start | bytes 2359296 | tf_op jit(solution)/shard_map/reduce_scatter | solution.py:30
Sparse Core Ops, SparseCore 0:
  60.1 41.8 reduce-scatter.1
where the time goes:
time: 111 us
  waiting for transfers between devices  62.1 us (56%)
  starting transfers between devices  19.1 us (17%)
  between operations  14.1 us (13%)
  other arithmetic  5.3 us (5%)
  local copies, waits for them, and re-layouts  5.06 us (5%)
  matrix products  5.03 us (5%)
    reduce_scatter x1, waiting for transfers between devices, on_device(): lax.psum_scatter(jnp.dot(weights, recoupled, preferred_element_type=jnp.f...  41.4 us
    all_to_all x1, waiting for transfers between devices, on_device(): lax.all_to_all(outbox.reshape(owners_count, capacity, hole_width), 'chan'...  20.7 us
    all_to_all x1, starting transfers between devices, on_device(): lax.all_to_all(outbox.reshape(owners_count, capacity, hole_width), 'chan'...  19.1 us
    dot_general x1, matrix products, on_device(): jnp.dot(weights, recoupled, preferred_element_type=jnp.float32)  5.03 us
  transfers between devices with their start and end apart: 2, of which 2 were waited for; matrix products, arithmetic and copies ran while one was open for 1% of the time, Pallas kernels for 0%

commit v1 on v0

--- a/solution.py
+++ b/solution.py
@@ -8,8 +8,8 @@
     ph_rows = t2_ph[0]
     owners = dest_owner[0]
     owners_count = lax.axis_size("chan")
-    slab_rows = ph_rows.shape[0]
-    hole_width = ph_rows.shape[1]
+    slabs = lax.axis_size("kred")
+    slab_rows, hole_width = ph_rows.shape
     capacity = 2 * slab_rows // owners_count
     matches = (owners[:, None] == jnp.arange(owners_count, dtype=jnp.int32)[None, :]).astype(
         jnp.int32
@@ -26,12 +26,18 @@
     )
     picked = source_owner[0] * capacity + source_slot[0]
     recoupled = arrived.reshape(owners_count * capacity, hole_width)[picked]
-    weights = ladder_v[0]
-    ladder = lax.psum_scatter(
-        jnp.dot(weights, recoupled, preferred_element_type=jnp.float32),
+    channel = lax.all_to_all(
+        jnp.broadcast_to(recoupled[None], (slabs, slab_rows, hole_width)),
         "kred",
-        scatter_dimension=0,
+        split_axis=0,
+        concat_axis=0,
         tiled=True,
+    ).reshape(slabs * slab_rows, hole_width)
+    ladder = lax.dot_general(
+        ladder_v[0],
+        channel,
+        (((0,), (0,)), ((), ())),
+        preferred_element_type=jnp.float32,
     )
     columns = jnp.arange(hole_width, dtype=jnp.int32)
     masked = jnp.where(columns[None, :] < hole_count[0], ladder, jnp.float32(0.0))

time: 111 us -> 90.6 us (0.82)
  the two profiles are of different devices: /device:TPU:2 before, /device:TPU:1 now
where the time goes in v1:
time: 90.6 us; the launch traced here: 90.2 us
  waiting for transfers between devices  49.3 us (54%)
  starting transfers between devices  26.8 us (30%)
  local copies, waits for them, and re-layouts  6.18 us (7%)
  other arithmetic  4.27 us (5%)
  matrix products  2.93 us (3%)
    all_to_all x1, waiting for transfers between devices, on_device(): lax.all_to_all(jnp.broadcast_to(recoupled[None], (slabs, slab_rows, hole_...  28.5 us
    all_to_all x1, waiting for transfers between devices, on_device(): lax.all_to_all(outbox.reshape(owners_count, capacity, hole_width), 'chan'...  20.8 us
    all_to_all x1, starting transfers between devices, on_device(): lax.all_to_all(outbox.reshape(owners_count, capacity, hole_width), 'chan'...  20 us
    all_to_all x1, starting transfers between devices, on_device(): lax.all_to_all(jnp.broadcast_to(recoupled[None], (slabs, slab_rows, hole_...  6.82 us
    dot_general x1, matrix products, on_device(): lax.dot_general(ladder_v[0], channel, (((0,), (0,)), ((), ())), preferred...  2.93 us
  transfers between devices with their start and end apart: 2, of which 2 were waited for; matrix products, arithmetic and copies ran while one was open for 1% of the time, Pallas kernels for 0%

profile of v1, /device:TPU:1, one launch (start us, length us, event | category | flops | bytes accessed | tf_op | source)
XLA Modules:
  0.0 90.2 jit_solution(12920599705314892698)
XLA Ops:
  0.0 0.0 copy-start
  0.0 0.7 fusion.14
  0.7 1.3 %reduce-window.6 = s32[96,4,128]{2,0,1:T(8,128)S(1)} reduce-window(s32[96,4,128]{2,0,1:T(8,128)S(1)} %fusion.14, s32[]{:T(128)} %constant.3.clone.1), window={size=1x1x128 pad=0_0x0_0x127_0}, to_apply=%region_0.0 | reduce-window | flops 6242304 | bytes 393220 | tf_op jit(solution)/shard_map/reduce-window
  2.0 0.2 slice_reduce_fusion
  2.3 0.8 fusion.13
  3.1 0.7 compare_select_fusion.1
  3.8 0.0 copy-done
  3.8 1.8 %scatter_custom_fusion = bf16[960,128]{1,0:T(8,128)(2,1)S(1)} fusion(s32[512]{0:T(512)S(1)} %bitcast.55, bf16[1,512,128]{2,1,0:T(8,128)(2,1)S(1)} %copy-done, bf16[]{:T(256)} %constant.5.clone.1), kind=kCustom, calls=%fused_computation.16 | custom fusion | bytes 376834 | tf_op jit(solution)/shard_map/scatter | solution.py:19
  5.6 0.8 reshape.93
  6.4 20.0 %all-to-all-start = ((bf16[96,10,128]{2,1,0:T(8,128)(2,1)}), bf16[96,10,128]{2,1,0:T(8,128)(2,1)S(1)}, u32[]{:S(2)}, u32[]{:S(2)}) async-start(bf16[96,10,128]{2,1,0:T(8,128)(2,1)} %reshape.93), calls=%async_computation | async-start | bytes 786432 | tf_op jit(solution)/shard_map/all_to_all | solution.py:20
  26.5 0.7 compare_select_fusion
  27.2 20.8 %all-to-all-done = bf16[96,10,128]{2,1,0:T(8,128)(2,1)S(1)} async-done(((bf16[96,10,128]{2,1,0:T(8,128)(2,1)}), bf16[96,10,128]{2,1,0:T(8,128)(2,1)S(1)}, u32[]{:S(2)}, u32[]{:S(2)}) %all-to-all-start) | async-done | bytes 245792 | tf_op jit(solution)/shard_map/all_to_all | solution.py:20
  48.0 0.1 reshape.94
  48.1 1.3 %gather_fusion = bf16[512,128]{1,0:T(8,128)(2,1)S(1)} fusion(bf16[960,128]{1,0:T(8,128)(2,1)S(1)} %reshape.94, s32[1024]{0:T(1024)S(1)} %pad_clamp_fusion), kind=kCustom, calls=%fused_computation | custom fusion | bytes 264192 | tf_op jit(solution)/shard_map/gather | solution.py:28
  49.4 1.1 %broadcast_in_dim.30 = bf16[8,512,128]{2,1,0:T(8,128)(2,1)} broadcast(bf16[512,128]{1,0:T(8,128)(2,1)S(1)} %gather_fusion), dimensions={1,2} | broadcast | bytes 1179648 | tf_op jit(solution)/shard_map/broadcast_in_dim | solution.py:30
  50.5 6.8 %all-to-all-start.1 = ((bf16[8,512,128]{2,1,0:T(8,128)(2,1)}), bf16[8,512,128]{2,1,0:T(8,128)(2,1)S(1)}, u32[]{:S(2)}, u32[]{:S(2)}) async-start(bf16[8,512,128]{2,1,0:T(8,128)(2,1)} %broadcast_in_dim.30), calls=%async_computation.1 | async-start | bytes 2097152 | tf_op jit(solution)/shard_map/all_to_all | solution.py:29
  58.0 28.5 %all-to-all-done.1 = bf16[8,512,128]{2,1,0:T(8,128)(2,1)S(1)} async-done(((bf16[8,512,128]{2,1,0:T(8,128)(2,1)}), bf16[8,512,128]{2,1,0:T(8,128)(2,1)S(1)}, u32[]{:S(2)}, u32[]{:S(2)}) %all-to-all-start.1) | async-done | bytes 1048608 | tf_op jit(solution)/shard_map/all_to_all | solution.py:29
  86.5 2.9 %fusion.8 = bf16[1,512,128]{1,2,0:T(8,128)(2,1)S(1)} fusion(bf16[4096,128]{1,0:T(8,128)(2,1)S(1)} %bitcast.50, bf16[1,4096,512]{2,1,0:T(8,128)(2,1)} %param.11, pred[128]{0:T(512)(128)(4,1)S(1)} %iota_compare_fusion.2), kind=kOutput, calls=%fused_computation.6 | convolution fusion | flops 537001984 | bytes 5374080 | tf_op jit(solution)/shard_map/dot_general | solution.py:36
  89.5 0.8 copy.9
  (4 shorter events, 0.1 us)
Async XLA Ops:
  0.0 3.8 %copy-start = (bf16[1,512,128]{2,1,0:T(8,128)(2,1)S(1)}, bf16[1,512,128]{2,1,0:T(8,128)(2,1)}, u32[]{:S(2)}) copy-start(bf16[1,512,128]{2,1,0:T(8,128)(2,1)} %param.6) | copy-start | bytes 393220
  6.4 41.5 %all-to-all-start = ((bf16[96,10,128]{2,1,0:T(8,128)(2,1)}), bf16[96,10,128]{2,1,0:T(8,128)(2,1)S(1)}, u32[]{:S(2)}, u32[]{:S(2)}) async-start(bf16[96,10,128]{2,1,0:T(8,128)(2,1)} %reshape.93), calls=%async_computation | async-start | bytes 786432 | tf_op jit(solution)/shard_map/all_to_all | solution.py:20
  50.5 36.0 %all-to-all-start.1 = ((bf16[8,512,128]{2,1,0:T(8,128)(2,1)}), bf16[8,512,128]{2,1,0:T(8,128)(2,1)S(1)}, u32[]{:S(2)}, u32[]{:S(2)}) async-start(bf16[8,512,128]{2,1,0:T(8,128)(2,1)} %broadcast_in_dim.30), calls=%async_computation.1 | async-start | bytes 2097152 | tf_op jit(solution)/shard_map/all_to_all | solution.py:29

commit v2 on v0

v2 whole, which is shorter than its diff:
```python
import functools

import jax
import jax.numpy as jnp
from jax import lax
from jax.experimental import pallas as pl
from jax.experimental.pallas import tpu as pltpu
from jax.sharding import PartitionSpec as P

BF16, F32 = jnp.bfloat16, jnp.float32
SMALL = pltpu.CompilerParams(vmem_limit_bytes=16 * 2**20)
BOTH_FIRST = (((0,), (0,)), ((), ()))


def one_hot(mask):
    return jnp.where(mask, 1.0, 0.0).astype(BF16)


def pack_rows(owners_count, capacity, owner_ref, rows_ref, outbox_ref):
    rows = rows_ref.shape[0]
    owner = owner_ref[...]
    match = owner == lax.broadcasted_iota(jnp.int32, (owners_count, rows), 0)
    row_at = lax.broadcasted_iota(jnp.int32, (rows, rows), 0)
    earlier = row_at < lax.broadcasted_iota(jnp.int32, (rows, rows), 1)
    counts = jnp.dot(one_hot(match), one_hot(earlier), preferred_element_type=F32)
    before = jnp.sum(jnp.where(match, counts, 0.0), axis=0, keepdims=True)
    target = owner * capacity + before.astype(jnp.int32)
    slots = lax.broadcasted_iota(jnp.int32, (owners_count * capacity, rows), 0)
    outbox_ref[...] = jnp.dot(
        one_hot(slots == target), rows_ref[...], preferred_element_type=F32
    ).astype(BF16)


def pick_rows(capacity, owner_ref, slot_ref, arrived_ref, copies_ref):
    picked = owner_ref[...] * capacity + slot_ref[...]
    slots = lax.broadcasted_iota(jnp.int32, (arrived_ref.shape[0], picked.shape[1]), 0)
    taken = lax.dot_general(
        arrived_ref[...], one_hot(slots == picked), BOTH_FIRST, preferred_element_type=F32
    ).astype(BF16)
    for k in range(copies_ref.shape[0]):
        copies_ref[k] = taken


def contract(hole_ref, channel_ref, weights_ref, out_ref):
    slabs, width, depth = channel_ref.shape
    total = jnp.dot(channel_ref[0], weights_ref[:depth, :], preferred_element_type=F32)
    for k in range(1, slabs):
        total += jnp.dot(
            channel_ref[k],
            weights_ref[k * depth : (k + 1) * depth, :],
            preferred_element_type=F32,
        )
    live = lax.broadcasted_iota(jnp.int32, total.shape, 0) < hole_ref[0]
    out_ref[...] = jnp.where(live, total, 0.0).T.astype(BF16)


def on_device(t2_ph, dest_owner, source_owner, source_slot, hole_count, ladder_v):
    owners_count, slabs = lax.axis_size("chan"), lax.axis_size("kred")
    _, slab_rows, width = t2_ph.shape
    capacity = 2 * slab_rows // owners_count
    slots = owners_count * capacity
    whole = pl.BlockSpec(memory_space=pltpu.VMEM)
    outbox = pl.pallas_call(
        functools.partial(pack_rows, owners_count, capacity),
        out_shape=jax.ShapeDtypeStruct((slots, width), BF16),
        in_specs=[whole] * 2,
        out_specs=whole,
        compiler_params=SMALL,
        name="pack_rows",
    )(dest_owner, t2_ph[0])
    arrived = lax.all_to_all(
        outbox.reshape(owners_count, capacity // 2, 2, width), "chan", 0, 0, tiled=True
    ).reshape(slots, width)
    copies = pl.pallas_call(
        functools.partial(pick_rows, capacity),
        out_shape=jax.ShapeDtypeStruct((slabs, width, slab_rows), BF16),
        in_specs=[whole] * 3,
        out_specs=whole,
        compiler_params=SMALL,
        name="pick_rows",
    )(source_owner, source_slot, arrived)
    channel = lax.all_to_all(copies, "kred", 0, 0, tiled=True)
    ladder = pl.pallas_call(
        contract,
        out_shape=jax.ShapeDtypeStruct((slab_rows, width), BF16),
        in_specs=[pl.BlockSpec(memory_space=pltpu.SMEM), whole, whole],
        out_specs=whole,
        compiler_params=SMALL,
        name="contract",
    )(hole_count, channel, ladder_v[0])
    return ladder[None]


def solution(mesh):
    placed = (
        P("chan", "kred", None),
        P("chan", "kred"),
        P("chan", "kred"),
        P("chan", "kred"),
        P("chan"),
        P("chan", None, "kred"),
    )
    return jax.shard_map(
        on_device, mesh=mesh, in_specs=placed, out_specs=P("chan", "kred", None), check_vma=False
    )
```

time: 111 us -> 82.5 us (0.74)
  the two profiles are of different devices: /device:TPU:2 before, /device:TPU:1 now
where the time goes in v2:
time: 82.5 us; the launch traced here: 82.2 us
  blocking collectives  37.6 us (46%)
  waiting for transfers between devices  28.5 us (35%)
  starting transfers between devices  6.82 us (8%)
  local copies, waits for them, and re-layouts  5.14 us (6%)
  Pallas kernels  3.42 us (4%)
    all_to_all x1, blocking collectives, on_device(): lax.all_to_all(outbox.reshape(owners_count, capacity // 2, 2, width), 'ch...  37.6 us
    all_to_all x1, waiting for transfers between devices, on_device(): channel = lax.all_to_all(copies, 'kred', 0, 0, tiled=True)  28.5 us
    all_to_all x1, starting transfers between devices, on_device(): channel = lax.all_to_all(copies, 'kred', 0, 0, tiled=True)  6.82 us
    unnamed x10, local copies, waits for them, and re-layouts  5.14 us
  transfers between devices with their start and end apart: 1, of which 1 were waited for; matrix products, arithmetic and copies ran while one was open for 0% of the time, Pallas kernels for 0%

profile of v2, /device:TPU:1, one launch (start us, length us, event | category | flops | bytes accessed | tf_op | source)
XLA Modules:
  0.0 82.2 jit_solution(1323063084412516248)
XLA Ops:
  0.0 0.0 copy-start.1
  0.0 0.9 %copy-done.1 = bf16[1,512,128]{2,1,0:T(8,128)(2,1)S(1)} copy-done((bf16[1,512,128]{2,1,0:T(8,128)(2,1)S(1)}, bf16[1,512,128]{2,1,0:T(8,128)(2,1)}, u32[]{:S(2)}) %copy-start.1) | copy-done | bytes 131096
  0.9 0.0 copy-start.2
  0.9 0.7 copy-done.2
  1.6 0.6 pack_rows.1
  2.2 37.6 %all_to_all.10 = bf16[96,5,2,128]{3,2,1,0:T(2,128)(2,1)S(1)} all-to-all(bf16[96,5,2,128]{3,2,1,0:T(2,128)(2,1)S(1)} %bitcast.7), channel_id=1, replica_groups=mesh['chan'=96,'kred'=8] {'chan'}, dimensions={0} | all-to-all | bytes 491520 | tf_op jit(solution)/shard_map/all_to_all | solution.py:71
  39.8 0.0 copy-start.3
  39.8 0.7 copy-done.3
  40.5 0.0 copy-start.4
  40.5 0.7 copy-done.4
  41.2 1.4 %pick_rows.1 = bf16[8,128,512]{2,1,0:T(8,128)(2,1)} custom-call(s32[1,512]{1,0:T(1,128)S(1)} %copy-done.3, s32[1,512]{1,0:T(1,128)S(1)} %copy-done.4, bf16[960,128]{1,0:T(8,128)(2,1)S(1)} %bitcast.6), custom_call_target="tpu_custom_call" | custom-call | tf_op jit(solution)/shard_map/pick_rows/pallas_call | solution.py:74
  42.5 6.8 %all-to-all-start.1 = ((bf16[8,128,512]{2,1,0:T(8,128)(2,1)}), bf16[8,128,512]{2,1,0:T(8,128)(2,1)S(1)}, u32[]{:S(2)}, u32[]{:S(2)}) async-start(bf16[8,128,512]{2,1,0:T(8,128)(2,1)} %pick_rows.1), calls=%async_computation.1 | async-start | bytes 2097152 | tf_op jit(solution)/shard_map/all_to_all | solution.py:82
  50.0 28.5 %all-to-all-done.1.channel_ref = bf16[8,128,512]{2,1,0:T(8,128)(2,1)S(1)} async-done(((bf16[8,128,512]{2,1,0:T(8,128)(2,1)}), bf16[8,128,512]{2,1,0:T(8,128)(2,1)S(1)}, u32[]{:S(2)}, u32[]{:S(2)}) %all-to-all-start.1) | async-done | bytes 1048608 | tf_op jit(solution)/shard_map/all_to_all | solution.py:82
  78.6 0.0 copy-start
  78.6 2.2 %copy-done = bf16[1,4096,512]{2,1,0:T(8,128)(2,1)S(1)} copy-done((bf16[1,4096,512]{2,1,0:T(8,128)(2,1)S(1)}, bf16[1,4096,512]{2,1,0:T(8,128)(2,1)}, u32[]{:S(2)}) %copy-start) | copy-done | bytes 4194328
  80.7 1.4 %contract.1 = bf16[512,128]{1,0:T(8,128)(2,1)} custom-call(s32[1]{0:T(128)S(6)} %copy.7.hole_ref, bf16[8,128,512]{2,1,0:T(8,128)(2,1)S(1)} %all-to-all-done.1.channel_ref, bf16[4096,512]{1,0:T(8,128)(2,1)S(1)} %bitcast.5), custom_call_target="tpu_custom_call" | custom-call | tf_op jit(solution)/shard_map/contract/pallas_call | solution.py:83
Async XLA Ops:
  0.0 0.9 %copy-start.1 = (bf16[1,512,128]{2,1,0:T(8,128)(2,1)S(1)}, bf16[1,512,128]{2,1,0:T(8,128)(2,1)}, u32[]{:S(2)}) copy-start(bf16[1,512,128]{2,1,0:T(8,128)(2,1)} %param.6) | copy-start | bytes 393220
  0.9 0.7 copy-start.2
  39.8 0.7 copy-start.3
  40.5 0.7 copy-start.4
  42.5 36.0 %all-to-all-start.1 = ((bf16[8,128,512]{2,1,0:T(8,128)(2,1)}), bf16[8,128,512]{2,1,0:T(8,128)(2,1)S(1)}, u32[]{:S(2)}, u32[]{:S(2)}) async-start(bf16[8,128,512]{2,1,0:T(8,128)(2,1)} %pick_rows.1), calls=%async_computation.1 | async-start | bytes 2097152 | tf_op jit(solution)/shard_map/all_to_all | solution.py:82
  78.6 2.2 %copy-start = (bf16[1,4096,512]{2,1,0:T(8,128)(2,1)S(1)}, bf16[1,4096,512]{2,1,0:T(8,128)(2,1)}, u32[]{:S(2)}) copy-start(bf16[1,4096,512]{2,1,0:T(8,128)(2,1)} %param.11) | copy-start | bytes 12582916
